TPU v7x, 32 devices: a whole 2x2x4 slice. The times are simulated.
32 devices in a mesh: dp: 8 (over z, x), seq: 4 (over y, core).
Axes of the slice: x: 2, y: 2, z: 4, core: 2. Of those that a mesh axis runs over, the one named last changes fastest.
Arguments:
- queries: bfloat16 [8, 512, 1024], P('dp', 'seq'), may hold values from -6 to 6
- key_vecs: bfloat16 [8, 512, 1024], P('dp', 'seq'), may hold values from -6 to 6
- value_vecs: bfloat16 [8, 512, 1024], P('dp', 'seq'), may hold values from -6 to 6
- residual_in: bfloat16 [8, 512, 1024], P('dp', 'seq'), may hold values from -8 to 8
- point_weight: bfloat16 [1024, 2048], P('seq'), may hold values from -0.5 to 0.5
- context_grad: bfloat16 [8, 512, 1024], P('dp', 'seq'), may hold values from -6 to 6
- depth_kernel: float32 [31, 1024], replicated, may hold values from -1 to 1
- norm_gain: float32 [1024], replicated, may hold values from 0.5 to 1.5
- norm_bias: float32 [1024], replicated, may hold values from -3 to 3
- conv_grad: bfloat16 [8, 512, 1024], P('dp', 'seq'), may hold values from -1.5 to 1.5
Outputs:
- context: bfloat16 [8, 512, 1024], P('dp', 'seq')
- conv_output: bfloat16 [8, 512, 1024], P('dp', 'seq')
- query_grad: bfloat16 [8, 512, 1024], P('dp', 'seq')
- key_grad: bfloat16 [8, 512, 1024], P('dp', 'seq')
- value_grad: bfloat16 [8, 512, 1024], P('dp', 'seq')
- input_grad: bfloat16 [8, 512, 2048], P('dp', 'seq')
- residual_grad: bfloat16 [8, 512, 1024], P('dp', 'seq')
- kernel_grad: float32 [31, 1024], replicated
- gain_grad: float32 [1024], replicated
- bias_grad: float32 [1024], replicated
All inputs are finite; a program needn't handle non-finite values.
Results may differ from a plain program's by a relative error of at most 0.0049.
The roundings to bfloat16 on the way count: a program that leaves them out, or rounds other values in their place, can miss the bound.
Values may be sent and summed in bfloat16 or wider, within the bound.
A program may use at most 64 MiB of HBM per device.

v0:
```python
import jax
import jax.numpy as jnp
from jax import lax
from jax.sharding import PartitionSpec as P

HEADS = 16


def from_behind(block, axis, distance):
    devices = range(lax.axis_size(axis))
    route = [(i - distance, i) for i in devices if i - distance in devices]
    return lax.ppermute(block, axis, route)


def block_probs(query_block, key_heads, scaling):
    scores = (
        jnp.einsum("qhd,khd->hqk", query_block, key_heads, preferred_element_type=jnp.float32)
        * scaling
    )
    shifted = jnp.exp(scores - jnp.max(scores, axis=2, keepdims=True))
    return shifted / jnp.sum(shifted, axis=2, keepdims=True)


def attend_forward(query_part, key_part, value_part, head_count):
    frames, channels = query_part.shape
    head_depth = channels // head_count
    scaling = head_depth ** (-0.5)
    query_heads = query_part.reshape(frames, head_count, head_depth)
    key_heads = key_part.reshape(frames, head_count, head_depth)
    value_heads = value_part.reshape(frames, head_count, head_depth)
    block_rows = min(512, frames)

    def one_block(running, index):
        query_block = lax.dynamic_slice_in_dim(query_heads, index * block_rows, block_rows, 0)
        rounded = block_probs(query_block, key_heads, scaling).astype(jnp.bfloat16)
        context = jnp.einsum(
            "hqk,khd->qhd", rounded, value_heads, preferred_element_type=jnp.float32
        ).astype(jnp.bfloat16)
        return (running, context)

    unused, blocks = lax.scan(
        one_block, jnp.zeros((), jnp.float32), jnp.arange(frames // block_rows)
    )
    return blocks.reshape(frames, channels)


def attend_backward(query_part, key_part, value_part, grad_part, context_part, head_count):
    frames, channels = query_part.shape
    head_depth = channels // head_count
    scaling = head_depth ** (-0.5)
    query_heads = query_part.reshape(frames, head_count, head_depth)
    key_heads = key_part.reshape(frames, head_count, head_depth)
    value_heads = value_part.reshape(frames, head_count, head_depth)
    grad_heads = grad_part.reshape(frames, head_count, head_depth)
    context_heads = context_part.reshape(frames, head_count, head_depth)
    block_rows = min(512, frames)

    def one_block(running, index):
        key_total, value_total = running
        start = index * block_rows
        query_block = lax.dynamic_slice_in_dim(query_heads, start, block_rows, 0)
        grad_block = lax.dynamic_slice_in_dim(grad_heads, start, block_rows, 0)
        context_block = lax.dynamic_slice_in_dim(context_heads, start, block_rows, 0)
        probabilities = block_probs(query_block, key_heads, scaling)
        rounded = probabilities.astype(jnp.bfloat16)
        row_dots = jnp.sum(
            grad_block.astype(jnp.float32) * context_block.astype(jnp.float32), axis=2
        )
        prob_grad = jnp.einsum(
            "qhd,khd->hqk", grad_block, value_heads, preferred_element_type=jnp.float32
        )
        score_grad = (probabilities * (prob_grad - row_dots.T[:, :, None]) * scaling).astype(
            jnp.bfloat16
        )
        query_grad = jnp.einsum(
            "hqk,khd->qhd", score_grad, key_heads, preferred_element_type=jnp.float32
        ).astype(jnp.bfloat16)
        key_total = key_total + jnp.einsum(
            "hqk,qhd->khd", score_grad, query_block, preferred_element_type=jnp.float32
        )
        value_total = value_total + jnp.einsum(
            "hqk,qhd->khd", rounded, grad_block, preferred_element_type=jnp.float32
        )
        return ((key_total, value_total), query_grad)

    empty = jnp.zeros((frames, head_count, head_depth), jnp.float32)
    totals, blocks = lax.scan(one_block, (empty, empty), jnp.arange(frames // block_rows))
    query_grad = blocks.reshape(frames, channels)
    key_grad = totals[0].astype(jnp.bfloat16).reshape(frames, channels)
    value_grad = totals[1].astype(jnp.bfloat16).reshape(frames, channels)
    return (query_grad, key_grad, value_grad)


def shards(
    queries,
    key_vecs,
    value_vecs,
    residual_in,
    point_weight,
    context_grad,
    depth_kernel,
    norm_gain,
    norm_bias,
    conv_grad,
):
    head_count = HEADS // lax.axis_size("seq")
    query_heads, key_heads, value_heads = (
        lax.all_to_all(queries, "seq", split_axis=2, concat_axis=1, tiled=True),
        lax.all_to_all(key_vecs, "seq", split_axis=2, concat_axis=1, tiled=True),
        lax.all_to_all(value_vecs, "seq", split_axis=2, concat_axis=1, tiled=True),
    )
    context_local = attend_forward(query_heads[0], key_heads[0], value_heads[0], head_count)
    context_out = lax.all_to_all(
        context_local[None], "seq", split_axis=1, concat_axis=2, tiled=True
    )
    taps = depth_kernel.shape[0]
    channels = depth_kernel.shape[1]
    span = taps - 1
    frames = residual_in.shape[1]
    mixed = (residual_in[0].astype(jnp.float32) + context_out[0].astype(jnp.float32)).astype(
        jnp.bfloat16
    )
    pre_conv = jnp.dot(
        mixed,
        lax.all_gather(point_weight, "seq", axis=0, tiled=True),
        preferred_element_type=jnp.float32,
    )
    conv_input = pre_conv.astype(jnp.bfloat16)[None]
    value_half = conv_input[:, :, :channels].astype(jnp.float32)
    gate_sig = jax.nn.sigmoid(conv_input[:, :, channels:].astype(jnp.float32))
    glu = (value_half * gate_sig).astype(jnp.bfloat16)
    earlier = from_behind(glu[:, frames - span :], "seq", 1)
    glu_wide = jnp.concatenate([earlier, glu], axis=1)
    glu_view = lax.optimization_barrier(glu_wide).astype(jnp.float32)
    depthwise = jnp.zeros((1, frames, channels), jnp.float32)
    for offset in range(taps):
        depthwise = depthwise + depth_kernel[offset] * glu_view[:, offset : offset + frames]
    average = jnp.mean(depthwise, axis=2, keepdims=True)
    centered = depthwise - average
    variance = jnp.mean(centered * centered, axis=2, keepdims=True)
    inverse = lax.rsqrt(variance + 1e-05)
    normed = centered * inverse
    affine = normed * norm_gain + norm_bias
    sig_affine = jax.nn.sigmoid(affine)
    conv_output = (affine * sig_affine).astype(jnp.bfloat16)
    affine_grad = conv_grad.astype(jnp.float32) * (sig_affine * (1.0 + affine * (1.0 - sig_affine)))
    gain_term = jnp.sum(affine_grad * normed, axis=(0, 1))
    bias_term = jnp.sum(affine_grad, axis=(0, 1))
    normed_grad = affine_grad * norm_gain
    depth_grad = inverse * (
        normed_grad
        - jnp.mean(normed_grad, axis=2, keepdims=True)
        - normed * jnp.mean(normed_grad * normed, axis=2, keepdims=True)
    )
    kernel_term = jnp.stack(
        [
            jnp.sum(depth_grad * glu_view[:, offset : offset + frames], axis=(0, 1))
            for offset in range(taps)
        ]
    )
    kernel_total, gain_total, bias_total = lax.psum(
        (kernel_term, gain_term, bias_term), ("dp", "seq")
    )
    recordings = lax.axis_size("dp")
    kernel_grad = kernel_total / recordings
    gain_grad = gain_total / recordings
    bias_grad = bias_total / recordings
    later = from_behind(depth_grad[:, :span], "seq", -1)
    grad_wide = jnp.concatenate([depth_grad, later], axis=1)
    glu_grad = jnp.zeros((1, frames, channels), jnp.float32)
    for offset in range(taps):
        begin = span - offset
        glu_grad = glu_grad + depth_kernel[offset] * grad_wide[:, begin : begin + frames]
    input_grad = jnp.concatenate(
        [glu_grad * gate_sig, glu_grad * value_half * gate_sig * (1.0 - gate_sig)], axis=2
    ).astype(jnp.bfloat16)
    slope_rows = input_grad[0]
    mixed_grad = jnp.einsum(
        "fc,dc->fd",
        slope_rows,
        lax.all_gather(point_weight, "seq", axis=0, tiled=True),
        preferred_element_type=jnp.float32,
    )
    residual_grad = (context_grad.astype(jnp.float32) + mixed_grad[None]).astype(jnp.bfloat16)
    grad_heads = lax.all_to_all(residual_grad, "seq", split_axis=2, concat_axis=1, tiled=True)
    query_grad, key_grad, value_grad = attend_backward(
        query_heads[0], key_heads[0], value_heads[0], grad_heads[0], context_local, head_count
    )
    query_out, key_out, value_out = (
        lax.all_to_all(query_grad[None], "seq", split_axis=1, concat_axis=2, tiled=True),
        lax.all_to_all(key_grad[None], "seq", split_axis=1, concat_axis=2, tiled=True),
        lax.all_to_all(value_grad[None], "seq", split_axis=1, concat_axis=2, tiled=True),
    )
    return (
        context_out,
        conv_output,
        query_out,
        key_out,
        value_out,
        input_grad,
        residual_grad,
        kernel_grad,
        gain_grad,
        bias_grad,
    )


def solution(mesh):
    in_specs = (
        P("dp", "seq", None),
        P("dp", "seq", None),
        P("dp", "seq", None),
        P("dp", "seq", None),
        P("seq", None),
        P("dp", "seq", None),
        P(),
        P(),
        P(),
        P("dp", "seq", None),
    )
    out_specs = (
        P("dp", "seq", None),
        P("dp", "seq", None),
        P("dp", "seq", None),
        P("dp", "seq", None),
        P("dp", "seq", None),
        P("dp", "seq", None),
        P("dp", "seq", None),
        P(),
        P(),
        P(),
    )
    return jax.shard_map(shards, mesh=mesh, in_specs=in_specs, out_specs=out_specs, check_vma=False)
```

profile of v0, /device:TPU:0, one launch (start us, length us, event | category | flops | bytes accessed | tf_op | source)
XLA Modules:
  0.0 264.9 jit_solution(9525014765251899373)
XLA Ops:
  12.9 4.2 %all-to-all-start = ((bf16[4,2,16384]{2,1,0:T(2,128)(2,1)}), bf16[4,2,16384]{2,1,0:T(2,128)(2,1)S(1)}, u32[]{:S(2)}, u32[]{:S(2)}) async-start(bf16[4,2,16384]{2,1,0:T(2,128)(2,1)} %reshape.213), calls=%async_computation | async-start | bytes 524288 | tf_op jit(solution)/shard_map/all_to_all | solution.py:108
  21.4 2.4 all-to-all-done
  23.9 3.4 %all-to-all-start.1 = ((bf16[4,2,16384]{2,1,0:T(2,128)(2,1)}), bf16[4,2,16384]{2,1,0:T(2,128)(2,1)S(1)}, u32[]{:S(2)}, u32[]{:S(2)}) async-start(bf16[4,2,16384]{2,1,0:T(2,128)(2,1)} %reshape.215), calls=%async_computation.1 | async-start | bytes 524288 | tf_op jit(solution)/shard_map/all_to_all | solution.py:109
  30.7 5.7 %all-to-all-done.1 = bf16[4,2,16384]{2,1,0:T(2,128)(2,1)S(1)} async-done(((bf16[4,2,16384]{2,1,0:T(2,128)(2,1)}), bf16[4,2,16384]{2,1,0:T(2,128)(2,1)S(1)}, u32[]{:S(2)}, u32[]{:S(2)}) %all-to-all-start.1) | async-done | bytes 262176 | tf_op jit(solution)/shard_map/all_to_all | solution.py:109
  36.4 3.4 %all-to-all-start.2 = ((bf16[4,2,16384]{2,1,0:T(2,128)(2,1)}), bf16[4,2,16384]{2,1,0:T(2,128)(2,1)S(1)}, u32[]{:S(2)}, u32[]{:S(2)}) async-start(bf16[4,2,16384]{2,1,0:T(2,128)(2,1)} %reshape.211), calls=%async_computation.2 | async-start | bytes 524288 | tf_op jit(solution)/shard_map/all_to_all | solution.py:110
  42.0 7.0 %all-to-all-done.2 = bf16[4,2,16384]{2,1,0:T(2,128)(2,1)S(1)} async-done(((bf16[4,2,16384]{2,1,0:T(2,128)(2,1)}), bf16[4,2,16384]{2,1,0:T(2,128)(2,1)S(1)}, u32[]{:S(2)}, u32[]{:S(2)}) %all-to-all-start.2) | async-done | bytes 262176 | tf_op jit(solution)/shard_map/all_to_all | solution.py:110
  49.6 3.5 %fusion.114 = (f32[4,512]{1,0:T(4,128)S(1)}, f32[4,512,512]{1,2,0:T(8,128)}) fusion(bf16[512,4,64]{0,2,1:T(8,128)(2,1)S(1)} %reshape_squeeze.15, bf16[512,4,64]{0,2,1:T(8,128)(2,1)S(1)} %reshape_squeeze.16), kind=kOutput, calls=%fused_computation.236 | convolution fusion | flops 137363968 | bytes 4726784 | tf_op jit(solution)/shard_map/while/body/eval_jaxpr/sub | solution.py:20
  53.1 2.8 %fusion.6 = bf16[4,512,512]{1,2,0:T(8,128)(2,1)S(1)} fusion(f32[4,512,512]{1,2,0:T(8,128)} %get-tuple-element.138, f32[4,512]{1,0:T(4,128)S(1)} %get-tuple-element.137), kind=kLoop, calls=%fused_computation.38 | loop fusion | flops 2097152 | bytes 6299648 | tf_op jit(solution)/shard_map/while/body/eval_jaxpr/convert_element_type | solution.py:35
  59.8 3.6 %all-to-all-start.3 = ((bf16[4,2,16384]{2,1,0:T(2,128)(2,1)}), bf16[4,2,16384]{2,1,0:T(2,128)(2,1)S(1)}, u32[]{:S(2)}, u32[]{:S(2)}) async-start(bf16[4,2,16384]{2,1,0:T(2,128)(2,1)} %reshape.217), calls=%async_computation.3 | async-start | bytes 524288 | tf_op jit(solution)/shard_map/all_to_all | solution.py:113
  64.2 5.1 %all-to-all-done.3 = bf16[4,2,16384]{2,1,0:T(2,128)(2,1)S(1)} async-done(((bf16[4,2,16384]{2,1,0:T(2,128)(2,1)}), bf16[4,2,16384]{2,1,0:T(2,128)(2,1)S(1)}, u32[]{:S(2)}, u32[]{:S(2)}) %all-to-all-start.3) | async-done | bytes 262176 | tf_op jit(solution)/shard_map/all_to_all | solution.py:113
  70.8 2.9 %fusion.4 = bf16[1,128,2048]{2,1,0:T(8,128)(2,1)S(1)} fusion(bf16[128,1024]{0,1:T(8,128)(2,1)S(1)} %fusion.105, bf16[1024,2048]{1,0:T(8,128)(2,1)} %all-gather.2.cloned.1.call-done), kind=kOutput, calls=%fused_computation.35 | convolution fusion | flops 537133056 | bytes 4980736 | tf_op jit(solution)/shard_map/dot_general | solution.py:123
  81.0 3.2 %fusion.111 = (f32[128]{0:T(128)S(1)}, f32[1,128,1024]{2,1,0:T(8,128)S(1)}) fusion(f32[1,158,1024]{2,1,0:T(8,128)S(1)} %convert_element_type.110, f32[1024]{0:T(1024)} %bitcast.253, f32[1024]{0:T(1024)} %bitcast.255, f32[1024]{0:T(1024)S(1)} %bitcast.197, f32[1024]{0:T(1024)S(1)} %bitcast.199, f32[1024]{0:T(1024)S(1)} %bitcast.201, f32[1024]{0:T(1024)} %bitcast.203, ...), kind=kLoop, calls=%fused_computation.233 | loop fusion | flops 8126336 | bytes 16904704 | tf_op jit(solution)/shard_map/reduce_sum | solution.py:138
  89.0 2.6 stack.127
  92.9 43.4 %all-reduce = (f32[1024]{0:T(1024)}, f32[1024]{0:T(1024)}) all-reduce(f32[1024]{0:T(1024)} %get-tuple-element.93, f32[1024]{0:T(1024)} %get-tuple-element.96), channel_id=1, replica_groups=mesh['dp'=8,'seq'=4] {'dp','seq'}, use_global_device_ids=true, to_apply=%region_40.41 | all-reduce | flops 2048 | bytes 16384 | tf_op jit(solution)/shard_map/psum | solution.py:161
  137.6 3.6 %multiply_convert_fusion.1 = (bf16[1,128,1024]{2,1,0:T(8,128)(2,1)S(1)}, f32[1,128,1024]{2,1,0:T(8,128)S(1)}) fusion(bf16[1,128,2048]{2,1,0:T(8,128)(2,1)S(1)} %fusion.4, f32[1,128,1024]{2,1,0:T(8,128)S(1)} %get-tuple-element.99, f32[1024]{0:T(1024)} %bitcast.254, f32[1,30,1024]{2,1,0:T(8,128)S(1)} %collective-permute-done.1, f32[1024]{0:T(1024)} %bitcast.256, ...), kind=kLoop, calls=%fused_computation.210 | loop fusion | flops 12713984 | bytes 1822720 | tf_op jit(solution)/shard_map/convert.7
  141.9 3.7 %fusion.8 = bf16[1,128,1024]{2,1,0:T(8,128)(2,1)S(1)} fusion(bf16[1024,2048]{1,0:T(8,128)(2,1)} %all-gather.2.cloned.1.call-done, bf16[128,1024]{1,0:T(8,128)(2,1)S(1)} %bitcast.164, bf16[128,1024]{1,0:T(8,128)(2,1)S(1)} %bitcast.163, bf16[1,128,1024]{2,1,0:T(8,128)(2,1)} %param.15), kind=kOutput, calls=%fused_computation.74 | convolution fusion | flops 538312704 | bytes 5242880 | tf_op jit(solution)/shard_map/fc,dc->fd/dot_general | solution.py:178
  146.1 3.0 %reduce.8 = bf16[1024,128]{1,0:T(8,128)(2,1)} reduce(bf16[1024,1,128]{2,1,0:T(2,128)(2,1)S(1)} %bitcast.180, bf16[]{:T(256)} %broadcast.119), dimensions={1}, to_apply=%bitcast.135.reduce_sub_computation | reduce | bytes 524290
  150.7 4.3 %all-to-all-start.4 = ((bf16[4,2,16384]{2,1,0:T(2,128)(2,1)}), bf16[4,2,16384]{2,1,0:T(2,128)(2,1)}, u32[]{:S(2)}, u32[]{:S(2)}) async-start(bf16[4,2,16384]{2,1,0:T(2,128)(2,1)} %reshape.219), calls=%async_computation.4 | async-start | bytes 524288 | tf_op jit(solution)/shard_map/all_to_all | solution.py:185
  155.0 61.4 %all-reduce.3.cloned.1.call-done = f32[31,1024]{1,0:T(8,128)} async-done(((f32[31,1024]{1,0:T(8,128)}), f32[31,1024]{1,0:T(8,128)}) %all-reduce.3.cloned.1.call-update) | async-done | bytes 126992 | tf_op jit(solution)/shard_map/psum | solution.py:161
  221.1 3.1 %multiply_convert_fusion = bf16[4,512,512]{1,2,0:T(8,128)(2,1)S(1)} fusion(bf16[512,4,64]{0,2,1:T(8,128)(2,1)S(1)} %reshape_squeeze.18, bf16[512,4,64]{0,2,1:T(8,128)(2,1)S(1)} %copy-done.7, f32[4,512]{1,0:T(4,128)S(1)} %bitcast.288, f32[4,512,512]{1,2,0:T(8,128)} %get-tuple-element.138, f32[4,512]{1,0:T(4,128)S(1)} %copy-done.14), kind=kOutput, calls=%fused_computation.30 | convolution fusion | flops 139460608 | bytes 6832128 | tf_op jit(solution)/shard_map/while/body/eval_jaxpr/qhd,khd->hqk/dot_general | solution.py:69
  224.7 2.3 reduce.11
  227.7 4.0 %all-to-all-start.7 = ((bf16[4,2,16384]{2,1,0:T(2,128)(2,1)}), bf16[4,2,16384]{2,1,0:T(2,128)(2,1)}, u32[]{:S(2)}, u32[]{:S(2)}) async-start(bf16[4,2,16384]{2,1,0:T(2,128)(2,1)} %reshape.225), calls=%async_computation.7 | async-start | bytes 524288 | tf_op jit(solution)/shard_map/all_to_all | solution.py:192
  237.8 3.4 %all-to-all-start.6 = ((bf16[4,2,16384]{2,1,0:T(2,128)(2,1)}), bf16[4,2,16384]{2,1,0:T(2,128)(2,1)S(1)}, u32[]{:S(2)}, u32[]{:S(2)}) async-start(bf16[4,2,16384]{2,1,0:T(2,128)(2,1)} %reshape.223), calls=%async_computation.6 | async-start | bytes 524288 | tf_op jit(solution)/shard_map/all_to_all | solution.py:191
  247.3 3.4 %all-to-all-start.5 = ((bf16[4,2,16384]{2,1,0:T(2,128)(2,1)}), bf16[4,2,16384]{2,1,0:T(2,128)(2,1)S(1)}, u32[]{:S(2)}, u32[]{:S(2)}) async-start(bf16[4,2,16384]{2,1,0:T(2,128)(2,1)} %reshape.221), calls=%async_computation.5 | async-start | bytes 524288 | tf_op jit(solution)/shard_map/all_to_all | solution.py:190
  (126 shorter events, 64.7 us)
Async XLA Ops:
  7.2 20.1 %copy-start.8 = (bf16[1,128,1024]{2,1,0:T(8,128)(2,1)S(1)}, bf16[1,128,1024]{2,1,0:T(8,128)(2,1)}, u32[]{:S(2)}) copy-start(bf16[1,128,1024]{2,1,0:T(8,128)(2,1)} %param.12) | copy-start | bytes 786436
  7.2 63.6 %all-gather.2.cloned.1.call-start = ((), (), s32[]{:S(2)}) async-start(), calls=%async_computation.8 | async-start | bytes 5242880 | tf_op jit(solution)/shard_map/all_gather | solution.py:125
  7.9 31.9 %copy-start.10 = (bf16[1,128,1024]{2,1,0:T(8,128)(2,1)S(1)}, bf16[1,128,1024]{2,1,0:T(8,128)(2,1)}, u32[]{:S(2)}) copy-start(bf16[1,128,1024]{2,1,0:T(8,128)(2,1)} %param.13) | copy-start | bytes 786436
  12.9 11.0 %all-to-all-start = ((bf16[4,2,16384]{2,1,0:T(2,128)(2,1)}), bf16[4,2,16384]{2,1,0:T(2,128)(2,1)S(1)}, u32[]{:S(2)}, u32[]{:S(2)}) async-start(bf16[4,2,16384]{2,1,0:T(2,128)(2,1)} %reshape.213), calls=%async_computation | async-start | bytes 524288 | tf_op jit(solution)/shard_map/all_to_all | solution.py:108
  23.9 12.5 %all-to-all-start.1 = ((bf16[4,2,16384]{2,1,0:T(2,128)(2,1)}), bf16[4,2,16384]{2,1,0:T(2,128)(2,1)S(1)}, u32[]{:S(2)}, u32[]{:S(2)}) async-start(bf16[4,2,16384]{2,1,0:T(2,128)(2,1)} %reshape.215), calls=%async_computation.1 | async-start | bytes 524288 | tf_op jit(solution)/shard_map/all_to_all | solution.py:109
  36.4 12.5 %all-to-all-start.2 = ((bf16[4,2,16384]{2,1,0:T(2,128)(2,1)}), bf16[4,2,16384]{2,1,0:T(2,128)(2,1)S(1)}, u32[]{:S(2)}, u32[]{:S(2)}) async-start(bf16[4,2,16384]{2,1,0:T(2,128)(2,1)} %reshape.211), calls=%async_computation.2 | async-start | bytes 524288 | tf_op jit(solution)/shard_map/all_to_all | solution.py:110
  41.3 11.8 %copy-start.5 = (bf16[512,4,64]{0,2,1:T(8,128)(2,1)}, bf16[512,4,64]{0,2,1:T(8,128)(2,1)S(1)}, u32[]{:S(2)}) copy-start(bf16[512,4,64]{0,2,1:T(8,128)(2,1)S(1)} %reshape_squeeze.15) | copy-start | bytes 786436
  42.0 11.1 %copy-start.4 = (bf16[512,4,64]{0,2,1:T(8,128)(2,1)}, bf16[512,4,64]{0,2,1:T(8,128)(2,1)S(1)}, u32[]{:S(2)}) copy-start(bf16[512,4,64]{0,2,1:T(8,128)(2,1)S(1)} %reshape_squeeze.16) | copy-start | bytes 786436
  49.6 6.3 %copy-start.6 = (bf16[512,4,64]{0,2,1:T(8,128)(2,1)}, bf16[512,4,64]{0,2,1:T(8,128)(2,1)S(1)}, u32[]{:S(2)}) copy-start(bf16[512,4,64]{0,2,1:T(8,128)(2,1)S(1)} %reshape_squeeze.17) | copy-start | bytes 786436
  55.9 7.6 %copy-start.11 = (f32[31,1024]{1,0:T(8,128)S(1)}, f32[31,1024]{1,0:T(8,128)}, u32[]{:S(2)}) copy-start(f32[31,1024]{1,0:T(8,128)} %param.16) | copy-start | bytes 380932
  59.8 9.4 %all-to-all-start.3 = ((bf16[4,2,16384]{2,1,0:T(2,128)(2,1)}), bf16[4,2,16384]{2,1,0:T(2,128)(2,1)S(1)}, u32[]{:S(2)}, u32[]{:S(2)}) async-start(bf16[4,2,16384]{2,1,0:T(2,128)(2,1)} %reshape.217), calls=%async_computation.3 | async-start | bytes 524288 | tf_op jit(solution)/shard_map/all_to_all | solution.py:113
  63.4 153.0 %all-reduce.3.cloned.1.call-start = ((), (), s32[]{:S(2)}) async-start(), calls=%async_computation.9 | async-start | bytes 262144 | tf_op jit(solution)/shard_map/psum | solution.py:161
  74.5 5.4 %collective-permute-start = (bf16[1,30,1024]{2,1,0:T(8,128)(2,1)}, bf16[1,30,1024]{2,1,0:T(8,128)(2,1)}, u32[]{:S(2)}, u32[]{:S(2)}) collective-permute-start(bf16[1,30,1024]{2,1,0:T(8,128)(2,1)} %slice.448), channel_id=1, source_target_pairs={{0,1},{1,2},{2,3},{4,5},{5,6},{6,7},{8,9},{9,10},{10,11},{12,13},{... | collective-permute-start | bytes 184328 | tf_op jit(solution)/shard_map/ppermute | solution.py:12
  80.9 3.5 %copy-start.9 = (bf16[1,128,1024]{2,1,0:T(8,128)(2,1)S(1)}, bf16[1,128,1024]{2,1,0:T(8,128)(2,1)}, u32[]{:S(2)}) copy-start(bf16[1,128,1024]{2,1,0:T(8,128)(2,1)} %param.19) | copy-start | bytes 786436
  81.0 3.5 %copy-start.12 = (f32[1024]{0:T(1024)S(1)}, f32[1024]{0:T(1024)}, u32[]{:S(2)}) copy-start(f32[1024]{0:T(1024)} %param.17) | copy-start | bytes 12292
  81.0 3.5 %copy-start.15 = (f32[1024]{0:T(1024)S(1)}, f32[1024]{0:T(1024)}, u32[]{:S(2)}) copy-start(f32[1024]{0:T(1024)} %param.18) | copy-start | bytes 12292
  91.6 46.0 %collective-permute-start.1 = (f32[1,30,1024]{2,1,0:T(8,128)}, f32[1,30,1024]{2,1,0:T(8,128)S(1)}, u32[]{:S(2)}, u32[]{:S(2)}) collective-permute-start(f32[1,30,1024]{2,1,0:T(8,128)} %slice.480), channel_id=1, source_target_pairs={{1,0},{2,1},{3,2},{5,4},{6,5},{7,6},{9,8},{10,9},{11,10},{13,12},{... | collective-permute-start | bytes 368648 | tf_op jit(solution)/shard_map/ppermute | solution.py:12
  145.6 73.6 %copy-start.2 = (bf16[1,128,1024]{2,1,0:T(8,128)(2,1)}, bf16[1,128,1024]{2,1,0:T(8,128)(2,1)S(1)}, u32[]{:S(2)}) copy-start(bf16[1,128,1024]{2,1,0:T(8,128)(2,1)S(1)} %fusion.8) | copy-start | bytes 786436
  145.7 75.4 %copy-start.14 = (f32[4,512]{1,0:T(4,128)S(1)}, f32[4,512]{1,0:T(4,128)}, u32[]{:S(2)}) copy-start(f32[4,512]{1,0:T(4,128)} %copy-done.13) | copy-start | bytes 24580
  150.7 67.2 %all-to-all-start.4 = ((bf16[4,2,16384]{2,1,0:T(2,128)(2,1)}), bf16[4,2,16384]{2,1,0:T(2,128)(2,1)}, u32[]{:S(2)}, u32[]{:S(2)}) async-start(bf16[4,2,16384]{2,1,0:T(2,128)(2,1)} %reshape.219), calls=%async_computation.4 | async-start | bytes 524288 | tf_op jit(solution)/shard_map/all_to_all | solution.py:185
  227.7 10.1 %all-to-all-start.7 = ((bf16[4,2,16384]{2,1,0:T(2,128)(2,1)}), bf16[4,2,16384]{2,1,0:T(2,128)(2,1)}, u32[]{:S(2)}, u32[]{:S(2)}) async-start(bf16[4,2,16384]{2,1,0:T(2,128)(2,1)} %reshape.225), calls=%async_computation.7 | async-start | bytes 524288 | tf_op jit(solution)/shard_map/all_to_all | solution.py:192
  233.4 17.2 %copy-start.1 = (bf16[1,128,1024]{2,1,0:T(8,128)(2,1)S(1)}, bf16[1,128,1024]{2,1,0:T(8,128)(2,1)}, u32[]{:S(2)}) copy-start(bf16[1,128,1024]{2,1,0:T(8,128)(2,1)} %copy-done) | copy-start | bytes 786436
  237.8 9.4 %all-to-all-start.6 = ((bf16[4,2,16384]{2,1,0:T(2,128)(2,1)}), bf16[4,2,16384]{2,1,0:T(2,128)(2,1)S(1)}, u32[]{:S(2)}, u32[]{:S(2)}) async-start(bf16[4,2,16384]{2,1,0:T(2,128)(2,1)} %reshape.223), calls=%async_computation.6 | async-start | bytes 524288 | tf_op jit(solution)/shard_map/all_to_all | solution.py:191
  247.3 9.4 %all-to-all-start.5 = ((bf16[4,2,16384]{2,1,0:T(2,128)(2,1)}), bf16[4,2,16384]{2,1,0:T(2,128)(2,1)S(1)}, u32[]{:S(2)}, u32[]{:S(2)}) async-start(bf16[4,2,16384]{2,1,0:T(2,128)(2,1)} %reshape.221), calls=%async_computation.5 | async-start | bytes 524288 | tf_op jit(solution)/shard_map/all_to_all | solution.py:190
  (4 other events, 9.0 us)
Sparse Core Ops, SparseCore 0:
  9.6 43.2 all-gather.1
  91.7 124.6 all-reduce.2
where the time goes:
time: 266 us; the launch traced here: 265 us
  waiting for transfers between devices  85.9 us (32%)
  blocking collectives  43.4 us (16%)
  other arithmetic  38.5 us (14%)
  starting transfers between devices  33.3 us (13%)
  local copies, waits for them, and re-layouts  30.8 us (12%)
  matrix products  18.3 us (7%)
  between operations  14.8 us (6%)
    psum x1, waiting for transfers between devices, shards(): lax.psum((kernel_term, gain_term, bias_term), ('dp', 'seq'))  61.4 us
    psum x1, blocking collectives, shards(): lax.psum((kernel_term, gain_term, bias_term), ('dp', 'seq'))  43.4 us
    unnamed x65, local copies, waits for them, and re-layouts  20.7 us
    unnamed x8, other arithmetic  18.7 us
    all_to_all x1, waiting for transfers between devices, shards(): lax.all_to_all(value_vecs, 'seq', split_axis=2, concat_axis=1, tiled=True)  6.95 us
    all_to_all x1, waiting for transfers between devices, shards(): lax.all_to_all(key_vecs, 'seq', split_axis=2, concat_axis=1, tiled=True)  5.69 us
  transfers between devices with their start and end apart: 12, of which 8 were waited for; matrix products, arithmetic and copies ran while one was open for 23% of the time, Pallas kernels for 0%

commit v1 on v0

--- a/solution.py
+++ b/solution.py
@@ -158,9 +158,8 @@
             for offset in range(taps)
         ]
     )
-    kernel_total, gain_total, bias_total = lax.psum(
-        (kernel_term, gain_term, bias_term), ("dp", "seq")
-    )
+    points_list = lambda panel: lax.psum(lax.psum(panel, axis_name="seq"), axis_name="dp")
+    kernel_total, gain_total, bias_total = points_list((kernel_term, gain_term, bias_term))
     recordings = lax.axis_size("dp")
     kernel_grad = kernel_total / recordings
     gain_grad = gain_total / recordings

time: 266 us -> 214 us (0.80)
  waiting for transfers between devices: 85.9 us -> 46.1 us
  blocking collectives: 43.4 us -> 32.3 us
  matrix products: 18.3 us -> 15.6 us
    psum x1 -> x2, waiting for transfers between devices: 61.4 us -> 17 us  [the longest x1 17 us: shards(): lax.psum(lax.psum(panel, axis_name='seq'), axis_name='dp')]
    psum x1 -> x2, blocking collectives: 43.4 us -> 32.3 us  [the longest x1 24.2 us: shards(): lax.psum(lax.psum(panel, axis_name='seq'), axis_name='dp')]
    all_to_all x1, waiting for transfers between devices: 0.01 us -> 4.1 us  [shards(): lax.all_to_all(residual_grad, 'seq', split_axis=2, concat_axis=1, tiled=T...]
  transfers between devices with their start and end apart: 12 -> 13, of which waited for: 8 -> 8; matrix products, arithmetic and copies ran while one was open for 23% -> 32% of each run, Pallas kernels for 0% -> 0%
where the time goes in v1:
time: 214 us; the launch traced here: 213 us
  waiting for transfers between devices  46.1 us (22%)
  other arithmetic  39.5 us (18%)
  starting transfers between devices  33.3 us (16%)
  blocking collectives  32.3 us (15%)
  local copies, waits for them, and re-layouts  31.4 us (15%)
  matrix products  15.6 us (7%)
  between operations  14.5 us (7%)
    psum x1, blocking collectives, shards(): lax.psum(lax.psum(panel, axis_name='seq'), axis_name='dp')  24.2 us
    unnamed x65, local copies, waits for them, and re-layouts  21.3 us
    unnamed x8, other arithmetic  18.7 us
    psum x1, waiting for transfers between devices, shards(): lax.psum(lax.psum(panel, axis_name='seq'), axis_name='dp')  17 us
    psum x1, blocking collectives, shards(): lax.psum(panel, axis_name='seq')  8.02 us
    all_to_all x1, waiting for transfers between devices, shards(): lax.all_to_all(value_vecs, 'seq', split_axis=2, concat_axis=1, tiled=True)  6.95 us
    all_to_all x1, waiting for transfers between devices, shards(): lax.all_to_all(key_vecs, 'seq', split_axis=2, concat_axis=1, tiled=True)  5.69 us
    all_to_all x1, waiting for transfers between devices, shards(): lax.all_to_all(context_local[None], 'seq', split_axis=1, concat_axis=2, t...  5.27 us
  transfers between devices with their start and end apart: 13, of which 8 were waited for; matrix products, arithmetic and copies ran while one was open for 32% of the time, Pallas kernels for 0%

profile of v1, /device:TPU:0, one launch (start us, length us, event | category | flops | bytes accessed | tf_op | source)
XLA Modules:
  0.0 212.7 jit_solution(5227789238799344264)
XLA Ops:
  12.9 4.2 %all-to-all-start = ((bf16[4,2,16384]{2,1,0:T(2,128)(2,1)}), bf16[4,2,16384]{2,1,0:T(2,128)(2,1)S(1)}, u32[]{:S(2)}, u32[]{:S(2)}) async-start(bf16[4,2,16384]{2,1,0:T(2,128)(2,1)} %reshape.213), calls=%async_computation | async-start | bytes 524288 | tf_op jit(solution)/shard_map/all_to_all | solution.py:108
  23.9 3.4 %all-to-all-start.1 = ((bf16[4,2,16384]{2,1,0:T(2,128)(2,1)}), bf16[4,2,16384]{2,1,0:T(2,128)(2,1)S(1)}, u32[]{:S(2)}, u32[]{:S(2)}) async-start(bf16[4,2,16384]{2,1,0:T(2,128)(2,1)} %reshape.215), calls=%async_computation.1 | async-start | bytes 524288 | tf_op jit(solution)/shard_map/all_to_all | solution.py:109
  30.7 5.7 %all-to-all-done.1 = bf16[4,2,16384]{2,1,0:T(2,128)(2,1)S(1)} async-done(((bf16[4,2,16384]{2,1,0:T(2,128)(2,1)}), bf16[4,2,16384]{2,1,0:T(2,128)(2,1)S(1)}, u32[]{:S(2)}, u32[]{:S(2)}) %all-to-all-start.1) | async-done | bytes 262176 | tf_op jit(solution)/shard_map/all_to_all | solution.py:109
  36.4 3.4 %all-to-all-start.2 = ((bf16[4,2,16384]{2,1,0:T(2,128)(2,1)}), bf16[4,2,16384]{2,1,0:T(2,128)(2,1)S(1)}, u32[]{:S(2)}, u32[]{:S(2)}) async-start(bf16[4,2,16384]{2,1,0:T(2,128)(2,1)} %reshape.211), calls=%async_computation.2 | async-start | bytes 524288 | tf_op jit(solution)/shard_map/all_to_all | solution.py:110
  42.0 7.0 %all-to-all-done.2 = bf16[4,2,16384]{2,1,0:T(2,128)(2,1)S(1)} async-done(((bf16[4,2,16384]{2,1,0:T(2,128)(2,1)}), bf16[4,2,16384]{2,1,0:T(2,128)(2,1)S(1)}, u32[]{:S(2)}, u32[]{:S(2)}) %all-to-all-start.2) | async-done | bytes 262176 | tf_op jit(solution)/shard_map/all_to_all | solution.py:110
  49.6 3.5 %fusion.114 = (f32[4,512]{1,0:T(4,128)S(1)}, f32[4,512,512]{1,2,0:T(8,128)}) fusion(bf16[512,4,64]{0,2,1:T(8,128)(2,1)S(1)} %reshape_squeeze.15, bf16[512,4,64]{0,2,1:T(8,128)(2,1)S(1)} %reshape_squeeze.16), kind=kOutput, calls=%fused_computation.236 | convolution fusion | flops 137363968 | bytes 4726784 | tf_op jit(solution)/shard_map/while/body/eval_jaxpr/sub | solution.py:20
  53.7 2.8 %fusion.6 = bf16[4,512,512]{1,2,0:T(8,128)(2,1)S(1)} fusion(f32[4,512,512]{1,2,0:T(8,128)} %get-tuple-element.140, f32[4,512]{1,0:T(4,128)S(1)} %get-tuple-element.139), kind=kLoop, calls=%fused_computation.38 | loop fusion | flops 2097152 | bytes 6299648 | tf_op jit(solution)/shard_map/while/body/eval_jaxpr/convert_element_type | solution.py:35
  60.4 3.6 %all-to-all-start.3 = ((bf16[4,2,16384]{2,1,0:T(2,128)(2,1)}), bf16[4,2,16384]{2,1,0:T(2,128)(2,1)S(1)}, u32[]{:S(2)}, u32[]{:S(2)}) async-start(bf16[4,2,16384]{2,1,0:T(2,128)(2,1)} %reshape.217), calls=%async_computation.3 | async-start | bytes 524288 | tf_op jit(solution)/shard_map/all_to_all | solution.py:113
  64.7 5.3 %all-to-all-done.3 = bf16[4,2,16384]{2,1,0:T(2,128)(2,1)S(1)} async-done(((bf16[4,2,16384]{2,1,0:T(2,128)(2,1)}), bf16[4,2,16384]{2,1,0:T(2,128)(2,1)S(1)}, u32[]{:S(2)}, u32[]{:S(2)}) %all-to-all-start.3) | async-done | bytes 262176 | tf_op jit(solution)/shard_map/all_to_all | solution.py:113
  71.5 2.9 %fusion.4 = bf16[1,128,2048]{2,1,0:T(8,128)(2,1)S(1)} fusion(bf16[128,1024]{0,1:T(8,128)(2,1)S(1)} %fusion.105, bf16[1024,2048]{1,0:T(8,128)(2,1)} %all-gather.2.cloned.1.call-done), kind=kOutput, calls=%fused_computation.35 | convolution fusion | flops 537133056 | bytes 4980736 | tf_op jit(solution)/shard_map/dot_general | solution.py:123
  81.7 3.2 %fusion.111 = (f32[128]{0:T(128)S(1)}, f32[1,128,1024]{2,1,0:T(8,128)S(1)}) fusion(f32[1,158,1024]{2,1,0:T(8,128)S(1)} %convert_element_type.110, f32[1024]{0:T(1024)} %bitcast.253, f32[1024]{0:T(1024)} %bitcast.255, f32[1024]{0:T(1024)S(1)} %bitcast.197, f32[1024]{0:T(1024)S(1)} %bitcast.199, f32[1024]{0:T(1024)S(1)} %bitcast.201, f32[1024]{0:T(1024)} %bitcast.203, ...), kind=kLoop, calls=%fused_computation.233 | loop fusion | flops 8126336 | bytes 16904704 | tf_op jit(solution)/shard_map/reduce_sum | solution.py:138
  89.7 2.7 %stack.127 = f32[31,1024]{1,0:T(8,128)} concatenate(f32[1,1024]{1,0:T(1,128)S(1)} %bitcast.287, f32[1,1024]{1,0:T(1,128)S(1)} %bitcast.286, f32[1,1024]{1,0:T(1,128)S(1)} %bitcast.285, f32[1,1024]{1,0:T(1,128)S(1)} %bitcast.284, f32[1,1024]{1,0:T(1,128)S(1)} %bitcast.283, f32[1,1024]{1,0:T(1,128)S(1)} %bitcast.282, f32[1,1024]{1,0:T(1,128)S(1)} %bitcast.281, ...), dimensions={0} | concatenate | bytes 253952 | tf_op jit(solution)/shard_map/stack | solution.py:155
  93.7 8.0 %all-reduce.1 = (f32[1024]{0:T(1024)}, f32[1024]{0:T(1024)}) all-reduce(f32[1024]{0:T(1024)} %get-tuple-element.93, f32[1024]{0:T(1024)} %get-tuple-element.96), channel_id=1, replica_groups=mesh['dp'=8,'seq'=4] {'seq'}, use_global_device_ids=true, to_apply=%region_41.42 | all-reduce | flops 2048 | bytes 16384 | tf_op jit(solution)/shard_map/psum | solution.py:161
  101.8 24.2 %all-reduce = (f32[1024]{0:T(1024)}, f32[1024]{0:T(1024)}) all-reduce(f32[1024]{0:T(1024)} %get-tuple-element.99, f32[1024]{0:T(1024)} %get-tuple-element.100), channel_id=1, replica_groups=mesh['dp'=8,'seq'=4] {'dp'}, use_global_device_ids=true, to_apply=%region_42.43 | all-reduce | flops 2048 | bytes 16384 | tf_op jit(solution)/shard_map/psum | solution.py:161
  127.3 3.6 %multiply_convert_fusion.1 = (bf16[1,128,1024]{2,1,0:T(8,128)(2,1)S(1)}, f32[1,128,1024]{2,1,0:T(8,128)S(1)}) fusion(bf16[1,128,2048]{2,1,0:T(8,128)(2,1)S(1)} %fusion.4, f32[1,128,1024]{2,1,0:T(8,128)S(1)} %get-tuple-element.101, f32[1024]{0:T(1024)} %bitcast.254, f32[1,30,1024]{2,1,0:T(8,128)S(1)} %collective-permute-done.1, f32[1024]{0:T(1024)} %bitcast.256, ...), kind=kLoop, calls=%fused_computation.210 | loop fusion | flops 12713984 | bytes 1822720 | tf_op jit(solution)/shard_map/convert.7
  131.7 3.7 %fusion.8 = bf16[1,128,1024]{2,1,0:T(8,128)(2,1)S(1)} fusion(bf16[1024,2048]{1,0:T(8,128)(2,1)} %all-gather.2.cloned.1.call-done, bf16[128,1024]{1,0:T(8,128)(2,1)S(1)} %bitcast.164, bf16[128,1024]{1,0:T(8,128)(2,1)S(1)} %bitcast.163, bf16[1,128,1024]{2,1,0:T(8,128)(2,1)} %param.15), kind=kOutput, calls=%fused_computation.74 | convolution fusion | flops 538312704 | bytes 5242880 | tf_op jit(solution)/shard_map/fc,dc->fd/dot_general | solution.py:177
  135.8 3.0 %reduce.8 = bf16[1024,128]{1,0:T(8,128)(2,1)} reduce(bf16[1024,1,128]{2,1,0:T(2,128)(2,1)S(1)} %bitcast.180, bf16[]{:T(256)} %broadcast.119), dimensions={1}, to_apply=%bitcast.135.reduce_sub_computation | reduce | bytes 524290
  140.5 4.3 %all-to-all-start.4 = ((bf16[4,2,16384]{2,1,0:T(2,128)(2,1)}), bf16[4,2,16384]{2,1,0:T(2,128)(2,1)}, u32[]{:S(2)}, u32[]{:S(2)}) async-start(bf16[4,2,16384]{2,1,0:T(2,128)(2,1)} %reshape.219), calls=%async_computation.4 | async-start | bytes 524288 | tf_op jit(solution)/shard_map/all_to_all | solution.py:184
  146.6 4.1 %all-to-all-done.4 = bf16[4,2,16384]{2,1,0:T(2,128)(2,1)} async-done(((bf16[4,2,16384]{2,1,0:T(2,128)(2,1)}), bf16[4,2,16384]{2,1,0:T(2,128)(2,1)}, u32[]{:S(2)}, u32[]{:S(2)}) %all-to-all-start.4) | async-done | bytes 262176 | tf_op jit(solution)/shard_map/all_to_all | solution.py:184
  153.1 3.1 %multiply_convert_fusion = bf16[4,512,512]{1,2,0:T(8,128)(2,1)S(1)} fusion(bf16[512,4,64]{0,2,1:T(8,128)(2,1)S(1)} %reshape_squeeze.18, bf16[512,4,64]{0,2,1:T(8,128)(2,1)S(1)} %copy-done.7, f32[4,512]{1,0:T(4,128)S(1)} %bitcast.288, f32[4,512,512]{1,2,0:T(8,128)} %get-tuple-element.140, f32[4,512]{1,0:T(4,128)S(1)} %copy-done.14), kind=kOutput, calls=%fused_computation.30 | convolution fusion | flops 139460608 | bytes 6832128 | tf_op jit(solution)/shard_map/while/body/eval_jaxpr/qhd,khd->hqk/dot_general | solution.py:69
  159.7 4.0 %all-to-all-start.7 = ((bf16[4,2,16384]{2,1,0:T(2,128)(2,1)}), bf16[4,2,16384]{2,1,0:T(2,128)(2,1)}, u32[]{:S(2)}, u32[]{:S(2)}) async-start(bf16[4,2,16384]{2,1,0:T(2,128)(2,1)} %reshape.225), calls=%async_computation.7 | async-start | bytes 524288 | tf_op jit(solution)/shard_map/all_to_all | solution.py:191
  169.8 3.4 %all-to-all-start.6 = ((bf16[4,2,16384]{2,1,0:T(2,128)(2,1)}), bf16[4,2,16384]{2,1,0:T(2,128)(2,1)S(1)}, u32[]{:S(2)}, u32[]{:S(2)}) async-start(bf16[4,2,16384]{2,1,0:T(2,128)(2,1)} %reshape.223), calls=%async_computation.6 | async-start | bytes 524288 | tf_op jit(solution)/shard_map/all_to_all | solution.py:190
  179.2 3.4 %all-to-all-start.5 = ((bf16[4,2,16384]{2,1,0:T(2,128)(2,1)}), bf16[4,2,16384]{2,1,0:T(2,128)(2,1)S(1)}, u32[]{:S(2)}, u32[]{:S(2)}) async-start(bf16[4,2,16384]{2,1,0:T(2,128)(2,1)} %reshape.221), calls=%async_computation.5 | async-start | bytes 524288 | tf_op jit(solution)/shard_map/all_to_all | solution.py:189
  182.7 17.0 %all-reduce.7.cloned.1.call-done = f32[31,1024]{1,0:T(8,128)} async-done(((f32[31,1024]{1,0:T(8,128)}), f32[31,1024]{1,0:T(8,128)}) %all-reduce.7.cloned.1.call-update) | async-done | bytes 126992 | tf_op jit(solution)/shard_map/psum | solution.py:161
  (130 shorter events, 68.7 us)
Async XLA Ops:
  7.2 20.1 %copy-start.8 = (bf16[1,128,1024]{2,1,0:T(8,128)(2,1)S(1)}, bf16[1,128,1024]{2,1,0:T(8,128)(2,1)}, u32[]{:S(2)}) copy-start(bf16[1,128,1024]{2,1,0:T(8,128)(2,1)} %param.12) | copy-start | bytes 786436
  7.2 64.4 %all-gather.2.cloned.1.call-start = ((), (), s32[]{:S(2)}) async-start(), calls=%async_computation.8 | async-start | bytes 5242880 | tf_op jit(solution)/shard_map/all_gather | solution.py:125
  7.9 31.9 %copy-start.10 = (bf16[1,128,1024]{2,1,0:T(8,128)(2,1)S(1)}, bf16[1,128,1024]{2,1,0:T(8,128)(2,1)}, u32[]{:S(2)}) copy-start(bf16[1,128,1024]{2,1,0:T(8,128)(2,1)} %param.13) | copy-start | bytes 786436
  12.9 11.0 %all-to-all-start = ((bf16[4,2,16384]{2,1,0:T(2,128)(2,1)}), bf16[4,2,16384]{2,1,0:T(2,128)(2,1)S(1)}, u32[]{:S(2)}, u32[]{:S(2)}) async-start(bf16[4,2,16384]{2,1,0:T(2,128)(2,1)} %reshape.213), calls=%async_computation | async-start | bytes 524288 | tf_op jit(solution)/shard_map/all_to_all | solution.py:108
  23.9 12.5 %all-to-all-start.1 = ((bf16[4,2,16384]{2,1,0:T(2,128)(2,1)}), bf16[4,2,16384]{2,1,0:T(2,128)(2,1)S(1)}, u32[]{:S(2)}, u32[]{:S(2)}) async-start(bf16[4,2,16384]{2,1,0:T(2,128)(2,1)} %reshape.215), calls=%async_computation.1 | async-start | bytes 524288 | tf_op jit(solution)/shard_map/all_to_all | solution.py:109
  36.4 12.5 %all-to-all-start.2 = ((bf16[4,2,16384]{2,1,0:T(2,128)(2,1)}), bf16[4,2,16384]{2,1,0:T(2,128)(2,1)S(1)}, u32[]{:S(2)}, u32[]{:S(2)}) async-start(bf16[4,2,16384]{2,1,0:T(2,128)(2,1)} %reshape.211), calls=%async_computation.2 | async-start | bytes 524288 | tf_op jit(solution)/shard_map/all_to_all | solution.py:110
  41.3 11.8 %copy-start.4 = (bf16[512,4,64]{0,2,1:T(8,128)(2,1)}, bf16[512,4,64]{0,2,1:T(8,128)(2,1)S(1)}, u32[]{:S(2)}) copy-start(bf16[512,4,64]{0,2,1:T(8,128)(2,1)S(1)} %reshape_squeeze.15) | copy-start | bytes 786436
  42.0 11.1 %copy-start.2 = (bf16[512,4,64]{0,2,1:T(8,128)(2,1)}, bf16[512,4,64]{0,2,1:T(8,128)(2,1)S(1)}, u32[]{:S(2)}) copy-start(bf16[512,4,64]{0,2,1:T(8,128)(2,1)S(1)} %reshape_squeeze.16) | copy-start | bytes 786436
  49.6 6.9 %copy-start.6 = (bf16[512,4,64]{0,2,1:T(8,128)(2,1)}, bf16[512,4,64]{0,2,1:T(8,128)(2,1)S(1)}, u32[]{:S(2)}) copy-start(bf16[512,4,64]{0,2,1:T(8,128)(2,1)S(1)} %reshape_squeeze.17) | copy-start | bytes 786436
  56.5 7.6 %copy-start.11 = (f32[31,1024]{1,0:T(8,128)S(1)}, f32[31,1024]{1,0:T(8,128)}, u32[]{:S(2)}) copy-start(f32[31,1024]{1,0:T(8,128)} %param.16) | copy-start | bytes 380932
  60.4 9.6 %all-to-all-start.3 = ((bf16[4,2,16384]{2,1,0:T(2,128)(2,1)}), bf16[4,2,16384]{2,1,0:T(2,128)(2,1)S(1)}, u32[]{:S(2)}, u32[]{:S(2)}) async-start(bf16[4,2,16384]{2,1,0:T(2,128)(2,1)} %reshape.217), calls=%async_computation.3 | async-start | bytes 524288 | tf_op jit(solution)/shard_map/all_to_all | solution.py:113
  64.0 63.3 %all-reduce.5.cloned.1.call-start = ((), (), s32[]{:S(2)}) async-start(), calls=%async_computation.9 | async-start | bytes 262144 | tf_op jit(solution)/shard_map/psum | solution.py:161
  75.3 5.4 %collective-permute-start = (bf16[1,30,1024]{2,1,0:T(8,128)(2,1)}, bf16[1,30,1024]{2,1,0:T(8,128)(2,1)}, u32[]{:S(2)}, u32[]{:S(2)}) collective-permute-start(bf16[1,30,1024]{2,1,0:T(8,128)(2,1)} %slice.448), channel_id=1, source_target_pairs={{0,1},{1,2},{2,3},{4,5},{5,6},{6,7},{8,9},{9,10},{10,11},{12,13},{... | collective-permute-start | bytes 184328 | tf_op jit(solution)/shard_map/ppermute | solution.py:12
  92.4 107.2 %all-reduce.7.cloned.1.call-start = ((), (), s32[]{:S(2)}) async-start(), calls=%async_computation.10 | async-start | bytes 262144 | tf_op jit(solution)/shard_map/psum | solution.py:161
  92.4 34.9 %collective-permute-start.1 = (f32[1,30,1024]{2,1,0:T(8,128)}, f32[1,30,1024]{2,1,0:T(8,128)S(1)}, u32[]{:S(2)}, u32[]{:S(2)}) collective-permute-start(f32[1,30,1024]{2,1,0:T(8,128)} %slice.480), channel_id=1, source_target_pairs={{1,0},{2,1},{3,2},{5,4},{6,5},{7,6},{9,8},{10,9},{11,10},{13,12},{... | collective-permute-start | bytes 368648 | tf_op jit(solution)/shard_map/ppermute | solution.py:12
  135.4 17.6 %copy-start.1 = (bf16[1,128,1024]{2,1,0:T(8,128)(2,1)}, bf16[1,128,1024]{2,1,0:T(8,128)(2,1)S(1)}, u32[]{:S(2)}) copy-start(bf16[1,128,1024]{2,1,0:T(8,128)(2,1)S(1)} %fusion.8) | copy-start | bytes 786436
  135.8 17.3 %copy-start.14 = (f32[4,512]{1,0:T(4,128)S(1)}, f32[4,512]{1,0:T(4,128)}, u32[]{:S(2)}) copy-start(f32[4,512]{1,0:T(4,128)} %copy-done.13) | copy-start | bytes 24580
  140.5 10.2 %all-to-all-start.4 = ((bf16[4,2,16384]{2,1,0:T(2,128)(2,1)}), bf16[4,2,16384]{2,1,0:T(2,128)(2,1)}, u32[]{:S(2)}, u32[]{:S(2)}) async-start(bf16[4,2,16384]{2,1,0:T(2,128)(2,1)} %reshape.219), calls=%async_computation.4 | async-start | bytes 524288 | tf_op jit(solution)/shard_map/all_to_all | solution.py:184
  146.6 6.5 %copy-start.7 = (bf16[512,4,64]{0,2,1:T(8,128)(2,1)S(1)}, bf16[512,4,64]{0,2,1:T(8,128)(2,1)}, u32[]{:S(2)}) copy-start(bf16[512,4,64]{0,2,1:T(8,128)(2,1)} %copy-done.6) | copy-start | bytes 786436
  153.1 10.6 %copy-start.5 = (bf16[512,4,64]{0,2,1:T(8,128)(2,1)S(1)}, bf16[512,4,64]{0,2,1:T(8,128)(2,1)}, u32[]{:S(2)}) copy-start(bf16[512,4,64]{0,2,1:T(8,128)(2,1)} %copy-done.4) | copy-start | bytes 786436
  156.2 17.0 %copy-start.3 = (bf16[512,4,64]{0,2,1:T(8,128)(2,1)S(1)}, bf16[512,4,64]{0,2,1:T(8,128)(2,1)}, u32[]{:S(2)}) copy-start(bf16[512,4,64]{0,2,1:T(8,128)(2,1)} %copy-done.2) | copy-start | bytes 786436
  159.7 10.1 %all-to-all-start.7 = ((bf16[4,2,16384]{2,1,0:T(2,128)(2,1)}), bf16[4,2,16384]{2,1,0:T(2,128)(2,1)}, u32[]{:S(2)}, u32[]{:S(2)}) async-start(bf16[4,2,16384]{2,1,0:T(2,128)(2,1)} %reshape.225), calls=%async_computation.7 | async-start | bytes 524288 | tf_op jit(solution)/shard_map/all_to_all | solution.py:191
  169.8 9.4 %all-to-all-start.6 = ((bf16[4,2,16384]{2,1,0:T(2,128)(2,1)}), bf16[4,2,16384]{2,1,0:T(2,128)(2,1)S(1)}, u32[]{:S(2)}, u32[]{:S(2)}) async-start(bf16[4,2,16384]{2,1,0:T(2,128)(2,1)} %reshape.223), calls=%async_computation.6 | async-start | bytes 524288 | tf_op jit(solution)/shard_map/all_to_all | solution.py:190
  179.2 25.6 %all-to-all-start.5 = ((bf16[4,2,16384]{2,1,0:T(2,128)(2,1)}), bf16[4,2,16384]{2,1,0:T(2,128)(2,1)S(1)}, u32[]{:S(2)}, u32[]{:S(2)}) async-start(bf16[4,2,16384]{2,1,0:T(2,128)(2,1)} %reshape.221), calls=%async_computation.5 | async-start | bytes 524288 | tf_op jit(solution)/shard_map/all_to_all | solution.py:189
  (5 other events, 11.7 us)
Sparse Core Ops, SparseCore 0:
  9.6 43.2 all-gather.1
  92.5 33.5 all-reduce.4
  129.9 69.6 all-reduce.6
